TPU v7x, 512 devices: a whole 4x8x8 slice. The times are simulated.
512 devices in a mesh: mach: 8 (over x, core), panel: 64 (over z, y).
Axes of the slice: x: 4, y: 8, z: 8, core: 2. Of those that a mesh axis runs over, the one named last changes fastest.
Arguments:
- adjoint: bfloat16 [8, 512, 4, 128], P('mach', 'panel'), may hold values from -6 to 6
- near_blocks: bfloat16 [8, 512, 8, 128, 128], P('mach', 'panel'), may hold values from -0.1875 to 0.1875
- pattern: int32 [512, 8], P('panel'), may hold values from 0 to 511, as said below
- trim_mask: int32 [8, 4], P('mach'), may hold values 0 or 1
- spline_blocks: bfloat16 [512, 6, 128, 128], P('panel'), may hold values from -0.21875 to 0.21875
- spline_owner: int32 [512, 6], P('panel'), may hold values from 0 to 63, all different within a row; in each aligned block of 8 rows (0 to 7, 8 to 15, ...) at most 2 rows name the same one
- spline_local: int32 [512, 6], P('panel'), may hold values from 0 to 7
- struct_inverse: bfloat16 [512, 128, 128], P('panel'), may hold values from -0.1875 to 0.1875
Outputs:
- panel_loads: float32 [8, 512, 4, 128], P('mach', 'panel')
- struct_adjoint: float32 [512, 4, 128], P('panel')
Inputs may be any that keep to these rules, and one draw needn't show every extreme that they name: `pattern`: entry 0 of row i is i itself; entry 1 is the mirror block (i + 256) mod 512; every other entry lies within 8 blocks of its row, and each row has one entry exactly 8 blocks away unless that falls outside the grid, where it is clipped to the end. `spline_owner`: the targets of one row are different owners; among the rows of one device no owner is named more than 2 times, a bound that some block reaches.
All inputs are finite; a program needn't handle non-finite values. No bound on the sum of `trim_mask` on one device may be relied on, other than what follows from the above.
Results may differ from a plain program's by a relative error of at most 0.004.
Values may be sent and summed in bfloat16 or wider, within the bound.
A program may use at most 64 MiB of HBM per device.

v0:
```python
import jax
import jax.numpy as jnp
from jax import lax
from jax.sharding import PartitionSpec as P


def pack_rows(flat_rows, owners_flat, locals_flat, keep, slot_index, owner_count, slots):
    destination = jnp.where(keep, owners_flat * slots + slot_index, -1)
    place_int = (
        destination[:, None] == jnp.arange(owner_count * slots, dtype=jnp.int32)[None, :]
    ).astype(jnp.int32)
    send_loads = jnp.dot(
        place_int.astype(jnp.float32).T,
        flat_rows,
        precision=lax.Precision.HIGHEST,
        preferred_element_type=jnp.float32,
    )
    send_loads = send_loads.reshape(owner_count, slots, flat_rows.shape[1])
    send_index = (jnp.sum(place_int * (locals_flat + 1)[:, None], axis=0) - 1).reshape(
        owner_count, slots
    )
    return (send_loads, send_index)


def on_device(
    adjoint,
    near_blocks,
    pattern,
    trim_mask,
    spline_blocks,
    spline_owner,
    spline_local,
    struct_inverse,
):
    block_count = adjoint.shape[1]
    rhs_count = adjoint.shape[2]
    width = adjoint.shape[3]
    owner_count = lax.axis_size("panel")
    spline_count = spline_blocks.shape[1]
    capacity = max(2, 2 * block_count * spline_count // owner_count)
    pool = lax.all_gather(adjoint[0], "panel", axis=0, tiled=True)
    picked = jnp.take(pool, pattern, axis=0)
    near = jnp.einsum("bkrp,bkpq->brq", picked, near_blocks[0], preferred_element_type=jnp.float32)
    loads = near * trim_mask[0].astype(jnp.float32)[None, :, None]
    rounded = loads.astype(jnp.bfloat16)
    owners_flat = spline_owner.reshape(-1)
    locals_flat = spline_local.reshape(-1)
    owner_hits = (owners_flat[:, None] == jnp.arange(owner_count, dtype=jnp.int32)[None, :]).astype(
        jnp.int32
    )
    earlier = jnp.cumsum(owner_hits, axis=0) - owner_hits
    slot_index = jnp.sum(earlier * owner_hits, axis=1)
    contrib = jnp.einsum(
        "brp,bspq->bsrq", rounded, spline_blocks, preferred_element_type=jnp.float32
    )
    flat_rows = contrib.reshape(block_count * spline_count, rhs_count * width)
    keep = slot_index >= 0
    send_loads, send_index = pack_rows(
        flat_rows, owners_flat, locals_flat, keep, slot_index, owner_count, capacity
    )
    got_loads, got_index = (
        lax.all_to_all(send_loads, "panel", split_axis=0, concat_axis=0, tiled=True),
        lax.all_to_all(send_index, "panel", split_axis=0, concat_axis=0, tiled=True),
    )
    struct_count = struct_inverse.shape[0]
    pick_rows = (
        got_index.reshape(-1)[None, :] == jnp.arange(struct_count, dtype=jnp.int32)[:, None]
    ).astype(jnp.float32)
    mine = jnp.dot(
        pick_rows,
        got_loads.reshape(owner_count * capacity, rhs_count * width),
        precision=lax.Precision.HIGHEST,
        preferred_element_type=jnp.float32,
    )
    total = lax.psum(mine, "mach")
    struct_rounded = total.reshape(struct_count, rhs_count, width).astype(jnp.bfloat16)
    struct_adjoint = jnp.einsum(
        "trp,tpq->trq", struct_rounded, struct_inverse, preferred_element_type=jnp.float32
    )
    return (loads[None], struct_adjoint)


def solution(mesh):
    in_specs = (
        P("mach", "panel", None, None),
        P("mach", "panel", None, None, None),
        P("panel", None),
        P("mach", None),
        P("panel", None, None, None),
        P("panel", None),
        P("panel", None),
        P("panel", None, None),
    )
    out_specs = (P("mach", "panel", None, None), P("panel", None, None))
    return jax.shard_map(
        on_device, mesh=mesh, in_specs=in_specs, out_specs=out_specs, check_vma=False
    )
```

profile of v0, /device:TPU:1, one launch (start us, length us, event | category | flops | bytes accessed | tf_op | source)
XLA Modules:
  0.0 122.1 jit_solution(18221186613864630665)
XLA Ops:
  0.6 0.0 copy-start
  0.6 0.9 eq.65
  1.6 0.1 fusion.16
  1.6 0.1 reduce_window_sum.11
  1.7 0.2 select_reduce_fusion.1
  1.9 0.7 broadcast_add_fusion
  2.6 0.1 add.49
  2.7 0.1 select_reduce_fusion
  2.8 0.7 sub.11
  3.5 17.1 %all-to-all-start = ((s32[64,1,2]{2,1,0:T(1,128)}), s32[64,1,2]{2,1,0:T(1,128)S(1)}, u32[]{:S(2)}, u32[]{:S(2)}) async-start(s32[64,1,2]{2,1,0:T(1,128)} %bitcast.8), calls=%async_computation | async-start | bytes 65536 | tf_op jit(solution)/shard_map/all_to_all | solution.py:63
  20.7 0.7 compare_select_fusion
  21.4 0.7 compare_and_fusion
  22.1 38.1 %all-gather = bf16[1,512,4,128]{3,2,0,1:T(4,128)(2,1)S(1)} all-gather(bf16[1,8,4,128]{3,2,0,1:T(4,128)(2,1)} %bitcast.37), channel_id=2, replica_groups=mesh['mach'=8,'panel'=64] {'panel'}, dimensions={1}, use_global_device_ids=true | all-gather | bytes 532480 | tf_op jit(solution)/shard_map/all_gather | solution.py:41
  60.1 0.1 reshape.85
  60.2 0.7 convert_bitcast_fusion.1
  60.9 0.7 gather_fusion
  61.6 0.0 copy-start.1
  61.6 0.4 fusion.5
  62.0 0.9 copy-done.1
  63.0 0.3 convolution_bitcast_fusion
  63.3 0.5 fusion.10
  63.8 0.9 copy.19
  64.7 0.0 all-to-all-done
  64.7 9.1 %all-to-all-start.1 = ((f32[64,2,512]{2,1,0:T(2,128)}), f32[64,2,512]{2,1,0:T(2,128)S(1)}, u32[]{:S(2)}, u32[]{:S(2)}) async-start(f32[64,2,512]{2,1,0:T(2,128)} %copy.19), calls=%async_computation.1 | async-start | bytes 524288 | tf_op jit(solution)/shard_map/all_to_all | solution.py:62
  73.9 0.5 broadcast.74
  74.4 0.7 reduce.3
  75.1 0.1 eq.72
  75.3 11.1 %all-to-all-done.1 = f32[64,2,512]{2,1,0:T(2,128)S(1)} async-done(((f32[64,2,512]{2,1,0:T(2,128)}), f32[64,2,512]{2,1,0:T(2,128)S(1)}, u32[]{:S(2)}, u32[]{:S(2)}) %all-to-all-start.1) | async-done | bytes 262176 | tf_op jit(solution)/shard_map/all_to_all | solution.py:62
  86.3 0.2 reshape.82
  86.5 0.2 fusion.22
  86.7 34.6 %psum.7 = bf16[8,512]{1,0:T(8,128)(2,1)S(1)} all-reduce(f32[8,512]{1,0:T(8,128)S(1)} %fusion.22), channel_id=1, replica_groups=mesh['mach'=8,'panel'=64] {'mach'}, use_global_device_ids=true, to_apply=%region_3.4 | all-reduce | flops 4096 | bytes 24576 | tf_op jit(solution)/shard_map/psum | solution.py:75
  121.3 0.8 fusion.19
  (10 shorter events, 0.1 us)
Async XLA Ops:
  0.6 60.9 %copy-start = (bf16[1,8,8,128,128]{4,3,2,1,0:T(8,128)(2,1)S(1)}, bf16[1,8,8,128,128]{4,3,2,1,0:T(8,128)(2,1)}, u32[]{:S(2)}) copy-start(bf16[1,8,8,128,128]{4,3,2,1,0:T(8,128)(2,1)} %param.9) | copy-start | bytes 6291460
  3.5 61.2 %all-to-all-start = ((s32[64,1,2]{2,1,0:T(1,128)}), s32[64,1,2]{2,1,0:T(1,128)S(1)}, u32[]{:S(2)}, u32[]{:S(2)}) async-start(s32[64,1,2]{2,1,0:T(1,128)} %bitcast.8), calls=%async_computation | async-start | bytes 65536 | tf_op jit(solution)/shard_map/all_to_all | solution.py:63
  61.6 1.4 %copy-start.1 = (bf16[8,6,128,128]{3,2,1,0:T(8,128)(2,1)S(1)}, bf16[8,6,128,128]{3,2,1,0:T(8,128)(2,1)}, u32[]{:S(2)}) copy-start(bf16[8,6,128,128]{3,2,1,0:T(8,128)(2,1)} %param.12) | copy-start | bytes 4718596
  63.0 23.7 %copy-start.3 = (f32[8,4,128]{2,1,0:T(4,128)}, f32[8,4,128]{2,1,0:T(4,128)S(1)}, u32[]{:S(2)}) copy-start(f32[8,4,128]{2,1,0:T(4,128)S(1)} %fusion.5) | copy-start | bytes 49156
  63.0 58.4 %copy-start.2 = (bf16[8,128,128]{2,1,0:T(8,128)(2,1)S(1)}, bf16[8,128,128]{2,1,0:T(8,128)(2,1)}, u32[]{:S(2)}) copy-start(bf16[8,128,128]{2,1,0:T(8,128)(2,1)} %param.15) | copy-start | bytes 786436
  64.7 21.6 %all-to-all-start.1 = ((f32[64,2,512]{2,1,0:T(2,128)}), f32[64,2,512]{2,1,0:T(2,128)S(1)}, u32[]{:S(2)}, u32[]{:S(2)}) async-start(f32[64,2,512]{2,1,0:T(2,128)} %copy.19), calls=%async_computation.1 | async-start | bytes 524288 | tf_op jit(solution)/shard_map/all_to_all | solution.py:62
where the time goes:
time: 124 us; the launch traced here: 122 us
  blocking collectives  72.7 us (59%)
  starting transfers between devices  26.3 us (21%)
  waiting for transfers between devices  11.1 us (9%)
  local copies, waits for them, and re-layouts  5.21 us (4%)
  other arithmetic  3.92 us (3%)
  matrix products  2.23 us (2%)
    all_gather x1, blocking collectives, on_device(): pool = lax.all_gather(adjoint[0], 'panel', axis=0, tiled=True)  38.1 us
    psum x1, blocking collectives, on_device(): total = lax.psum(mine, 'mach')  34.6 us
    all_to_all x1, starting transfers between devices, on_device(): lax.all_to_all(send_index, 'panel', split_axis=0, concat_axis=0, tiled=True)  17.1 us
    all_to_all x1, waiting for transfers between devices, on_device(): lax.all_to_all(send_loads, 'panel', split_axis=0, concat_axis=0, tiled=True)  11.1 us
    all_to_all x1, starting transfers between devices, on_device(): lax.all_to_all(send_loads, 'panel', split_axis=0, concat_axis=0, tiled=True)  9.13 us
  transfers between devices with their start and end apart: 2, of which 1 were waited for; matrix products, arithmetic and copies ran while one was open for 5% of the time, Pallas kernels for 0%

commit v1 on v0

v1 whole, which is shorter than its diff:
```python
import jax
import jax.numpy as jnp
from jax import lax
from jax.experimental import pallas as pl
from jax.experimental.pallas import tpu as pltpu
from jax.sharding import PartitionSpec as P

MESH = pl.DeviceIdType.MESH
F32 = jnp.float32
BF16 = jnp.bfloat16
MACHS = 8
PANELS = 64
RING = 8
ROWS = 8
NNZ = 8
TARGETS = 6
RHS = 4
CAP = 2
LANES = TARGETS * ROWS * RHS
SLOTS = PANELS * CAP * RHS


def iota(shape, axis):
    return lax.broadcasted_iota(jnp.int32, shape, axis)


def ones_where(cond):
    return jnp.where(cond, 1.0, 0.0).astype(BF16)


def kernel(
    adj_ref,
    near_hbm,
    pat_ref,
    mask_ref,
    spline_hbm,
    own_ref,
    loc_ref,
    inv_hbm,
    loads_ref,
    struct_ref,
    near_ref,
    spline_ref,
    inv_ref,
    pool,
    mirror,
    near_acc,
    mach_buf,
    place,
    pick,
    tab,
    ytab,
    ycomp,
    ztab,
    send_buf,
    recv_buf,
    load_sem,
    halo_send,
    halo_recv,
    ring_send,
    ring_recv,
    mach_send,
    mach_recv,
    all_send,
    all_recv,
):
    m = lax.axis_index("mach")
    p = lax.axis_index("panel")
    z = p // RING
    y = p % RING

    loads = [
        pltpu.make_async_copy(near_hbm, near_ref, load_sem.at[0]),
        pltpu.make_async_copy(spline_hbm, spline_ref, load_sem.at[1]),
        pltpu.make_async_copy(inv_hbm, inv_ref, load_sem.at[2]),
    ]
    barrier = pltpu.get_barrier_semaphore()

    def row_peer(j):
        return (m, z * RING + (y + j) % RING)

    def column_peer(j):
        return (m, ((z + j) % RING) * RING + y)

    def mach_peer(j):
        return ((m + j) % MACHS, p)

    right = (m, (p + 1) % PANELS)
    left = (m, (p + PANELS - 1) % PANELS)
    opposite = (m, (p + PANELS // 2) % PANELS)

    peers = [left, right]
    for j in range(1, RING):
        peers += [row_peer(j), column_peer(j), mach_peer(j)]
    for peer in peers:
        pl.semaphore_signal(barrier, inc=1, device_id=peer, device_id_type=MESH)
    for copy in loads:
        copy.start()

    own = own_ref[...].astype(F32)
    loc = loc_ref[...].astype(F32)
    lane = iota((ROWS, LANES), 1)
    sub = iota((ROWS, LANES), 0)
    lane_s = lane // (ROWS * RHS)
    lane_i = (lane // RHS) % ROWS
    own_rows = jnp.zeros((ROWS, LANES), F32)
    loc_rows = jnp.zeros((ROWS, LANES), F32)
    for s in range(TARGETS):
        own_rows = jnp.where(lane_s == s, own[:, s : s + 1], own_rows)
        loc_rows = jnp.where(lane_s == s, loc[:, s : s + 1], loc_rows)
    mine = sub == lane_i
    own_lane = jnp.sum(jnp.where(mine, own_rows, 0.0), axis=0, keepdims=True)
    loc_lane = jnp.sum(jnp.where(mine, loc_rows, 0.0), axis=0, keepdims=True)
    same = jnp.zeros((ROWS, LANES), F32)
    for s in range(TARGETS):
        same = same + jnp.where(own[:, s : s + 1] == own_lane, 1.0, 0.0)
    slot = jnp.sum(jnp.where(sub < lane_i, same, 0.0), axis=0, keepdims=True)
    dest = own_lane * CAP + slot
    lane_r = (iota((1, LANES), 1) % RHS).astype(F32)
    place[...] = ones_where(iota((SLOTS, LANES), 0).astype(F32) == dest * RHS + lane_r)
    chosen = ones_where(iota((PANELS * CAP, LANES), 0).astype(F32) == dest)
    weights = jnp.broadcast_to(
        jnp.where(lane_r == 0.0, loc_lane + 1.0, 0.0), (ROWS, LANES)
    ).astype(BF16)
    tab[...] = lax.dot_general(
        weights, chosen, (((1,), (1,)), ((), ())), preferred_element_type=F32
    )
    pool[ROWS : 2 * ROWS] = adj_ref[...]

    pl.semaphore_wait(barrier, len(peers))

    def send(src, dst, send_sem, recv_sem, peer):
        copy = pltpu.make_async_remote_copy(
            src_ref=src,
            dst_ref=dst,
            send_sem=send_sem,
            recv_sem=recv_sem,
            device_id=peer,
            device_id_type=MESH,
        )
        copy.start()
        return copy

    def drain(ref, sem):
        pltpu.make_async_copy(ref, ref, sem).wait()

    halos = [
        send(adj_ref, mirror, halo_send.at[0], halo_recv.at[0], opposite),
        send(adj_ref, pool.at[pl.ds(0, ROWS)], halo_send.at[1], halo_recv.at[1], right),
        send(adj_ref, pool.at[pl.ds(2 * ROWS, ROWS)], halo_send.at[2], halo_recv.at[2], left),
    ]
    for j in range(1, RING):
        send(tab, ytab.at[y], ring_send.at[0], ring_recv.at[0], row_peer(j))
    ytab[y] = tab[...]

    loads[0].wait()
    halos[1].wait_recv()
    halos[2].wait_recv()
    for i in range(ROWS):
        picked = [
            pool[jnp.clip(pat_ref[i, k] - p * ROWS + ROWS, 0, 3 * ROWS - 1)]
            for k in range(2, NNZ)
        ]
        near_acc[RHS * i : RHS * (i + 1), :] = jnp.dot(
            pool[ROWS + i], near_ref[i, 0], preferred_element_type=F32
        ) + jnp.dot(
            jnp.concatenate(picked, axis=1),
            near_ref[i, 2:NNZ].reshape((NNZ - 2) * 128, 128),
            preferred_element_type=F32,
        )

    drain(ytab.at[pl.ds(0, RING - 1)], ring_recv.at[0])
    sub8 = iota((RING, 128), 0)
    comp = jnp.zeros((RING, 128), F32)
    for j in range(RING):
        comp = jnp.where(sub8 == j, ytab[j], comp)
    ycomp[...] = comp
    for j in range(1, RING):
        send(ycomp, ztab.at[z], ring_send.at[1], ring_recv.at[1], column_peer(j))
    ztab[z] = ycomp[...]

    row32 = iota((ROWS * RHS, 1), 0)
    gate = jnp.zeros((ROWS * RHS, 1), F32)
    for r in range(RHS):
        gate = jnp.where(row32 % RHS == r, mask_ref[0, r].astype(F32), gate)

    halos[0].wait_recv()
    for i in range(ROWS):
        near_acc[RHS * i : RHS * (i + 1), :] += jnp.dot(
            mirror[i], near_ref[i, 1], preferred_element_type=F32
        )
    masked = near_acc[...] * gate
    loads_ref[...] = masked
    mach_buf[m] = masked.astype(BF16)
    for j in range(1, MACHS):
        send(mach_buf.at[m], mach_buf.at[m], mach_send, mach_recv, mach_peer(j))

    drain(ztab.at[pl.ds(0, RING - 1)], ring_recv.at[1])
    lane5 = iota((128, SLOTS), 1)
    wanted = ones_where(iota((128, SLOTS), 0) == p * CAP + (lane5 // RHS) % CAP)
    blocks = jnp.dot(
        ztab[...].reshape(PANELS, 128).astype(BF16), wanted, preferred_element_type=F32
    )
    from_panel = iota((PANELS, SLOTS), 0) == iota((PANELS, SLOTS), 1) // (CAP * RHS)
    block_lane = jnp.sum(jnp.where(from_panel, blocks, 0.0), axis=0, keepdims=True)
    row5 = iota((ROWS * RHS, SLOTS), 0)
    col5 = iota((ROWS * RHS, SLOTS), 1)
    pick[...] = ones_where(
        (block_lane == (row5 // RHS + 1).astype(F32)) & (col5 % RHS == row5 % RHS)
    )

    loads[1].wait()
    drain(mach_buf.at[pl.ds(0, MACHS - 1)], mach_recv)
    total = mach_buf[0].astype(F32)
    for j in range(1, MACHS):
        total = total + mach_buf[j].astype(F32)
    high = total.astype(BF16).astype(F32)
    both = jnp.concatenate([high, total - high], axis=0)
    row64 = (iota((2 * ROWS * RHS, 128), 0) // RHS) % ROWS
    spread = jnp.concatenate(
        [jnp.where(row64 == i, both, 0.0).astype(BF16) for i in range(ROWS)], axis=1
    )
    contrib = []
    for s in range(TARGETS):
        out = jnp.dot(
            spread,
            spline_ref[:, s].reshape(ROWS * 128, 128),
            preferred_element_type=F32,
        )
        contrib.append((out[: ROWS * RHS] + out[ROWS * RHS :]).astype(BF16))
    packed = jnp.dot(
        place[...], jnp.concatenate(contrib, axis=0), preferred_element_type=F32
    )
    send_buf[...] = packed.astype(BF16).reshape(PANELS, CAP * RHS, 128)

    def post(j, carry):
        peer = (p + PANELS // 2 + j) % PANELS

        @pl.when(peer != p)
        def _():
            send(send_buf.at[peer], recv_buf.at[p], all_send, all_recv, (m, peer))

        return carry

    lax.fori_loop(0, PANELS, post, 0)
    recv_buf[p] = send_buf[p]

    loads[2].wait()
    drain(recv_buf.at[pl.ds(0, PANELS - 1)], all_recv)
    found = jnp.dot(
        pick[...],
        recv_buf[...].reshape(SLOTS, 128),
        preferred_element_type=F32,
    )
    row_block = iota((ROWS * RHS, 128), 0) // RHS
    spread = jnp.concatenate(
        [jnp.where(row_block == t, found, 0.0).astype(BF16) for t in range(ROWS)], axis=1
    )
    struct_ref[...] = jnp.dot(
        spread, inv_ref[...].reshape(ROWS * 128, 128), preferred_element_type=F32
    )

    for copy in halos:
        copy.wait_send()
    for stage, ref in enumerate((ytab, ztab)):
        drain(ref.at[pl.ds(0, RING - 1)], ring_send.at[stage])
    drain(mach_buf.at[pl.ds(0, MACHS - 1)], mach_send)
    drain(send_buf.at[pl.ds(0, PANELS - 1)], all_send)


def on_device(adjoint, near, pattern, mask, spline, owner, local, inverse):
    vmem = pl.BlockSpec(memory_space=pltpu.VMEM)
    smem = pl.BlockSpec(memory_space=pltpu.SMEM)
    hbm = pl.BlockSpec(memory_space=pl.ANY)
    rows = ROWS * RHS
    dma = pltpu.SemaphoreType.DMA
    loads, struct = pl.pallas_call(
        kernel,
        out_shape=(
            jax.ShapeDtypeStruct((rows, 128), F32),
            jax.ShapeDtypeStruct((rows, 128), F32),
        ),
        in_specs=[vmem, hbm, smem, smem, hbm, vmem, vmem, hbm],
        out_specs=(vmem, vmem),
        scratch_shapes=[
            pltpu.VMEM((ROWS, NNZ, 128, 128), BF16),
            pltpu.VMEM((ROWS, TARGETS, 128, 128), BF16),
            pltpu.VMEM((ROWS, 128, 128), BF16),
            pltpu.VMEM((3 * ROWS, RHS, 128), BF16),
            pltpu.VMEM((ROWS, RHS, 128), BF16),
            pltpu.VMEM((rows, 128), F32),
            pltpu.VMEM((MACHS, rows, 128), BF16),
            pltpu.VMEM((SLOTS, LANES), BF16),
            pltpu.VMEM((rows, SLOTS), BF16),
            pltpu.VMEM((RING, 128), F32),
            pltpu.VMEM((RING, RING, 128), F32),
            pltpu.VMEM((RING, 128), F32),
            pltpu.VMEM((RING, RING, 128), F32),
            pltpu.VMEM((PANELS, CAP * RHS, 128), BF16),
            pltpu.VMEM((PANELS, CAP * RHS, 128), BF16),
            dma((3,)),
            dma((3,)),
            dma((3,)),
            dma((2,)),
            dma((2,)),
            dma,
            dma,
            dma,
            dma,
        ],
        compiler_params=pltpu.CompilerParams(collective_id=0, has_side_effects=True),
        name="load_transfer",
    )(adjoint[0], near[0], pattern, mask, spline, owner, local, inverse)
    return loads.reshape(1, ROWS, RHS, 128), struct.reshape(ROWS, RHS, 128)


def solution(mesh):
    in_specs = (
        P("mach", "panel", None, None),
        P("mach", "panel", None, None, None),
        P("panel", None),
        P("mach", None),
        P("panel", None, None, None),
        P("panel", None),
        P("panel", None),
        P("panel", None, None),
    )
    out_specs = (P("mach", "panel", None, None), P("panel", None, None))
    return jax.shard_map(
        on_device, mesh=mesh, in_specs=in_specs, out_specs=out_specs, check_vma=False
    )
```

time: 124 us -> 38.1 us (0.31); the launches traced: 122 us -> 37.7 us
  blocking collectives: 72.7 us -> 0 us
  Pallas kernels: 0 us -> 34.5 us
  starting transfers between devices: 26.3 us -> 0 us
  waiting for transfers between devices: 11.1 us -> 0 us
  other arithmetic: 3.92 us -> 0 us
  local copies, waits for them, and re-layouts: 5.21 us -> 2.65 us
  matrix products: 2.23 us -> 0 us
    all_gather x1 -> x0, blocking collectives: 38.1 us -> none  [on_device(): pool = lax.all_gather(adjoint[0], 'panel', axis=0, tiled=True)]
    psum x1 -> x0, blocking collectives: 34.6 us -> none  [on_device(): total = lax.psum(mine, 'mach')]
    pallas_call x0 -> x1, Pallas kernels: none -> 34.5 us  [on_device(): pl.pallas_call(kernel, out_shape=(jax.ShapeDtypeStruct((rows, 128), F32),...]
    all_to_all x2 -> x0, starting transfers between devices: 26.3 us -> none  [the longest x1 17.1 us: on_device(): lax.all_to_all(send_index, 'panel', split_axis=0, concat_axis=0, tiled=True)]
    all_to_all x2 -> x0, waiting for transfers between devices: 11.1 us -> none  [the longest x1 11.1 us: on_device(): lax.all_to_all(send_loads, 'panel', split_axis=0, concat_axis=0, tiled=True)]
    dot_general x5 -> x0, matrix products: 2.23 us -> none  [the longest x1 0.79 us: on_device(): jnp.einsum('trp,tpq->trq', struct_rounded, struct_inverse, preferred_elem...]
    unnamed x8 -> x2, local copies, waits for them, and re-layouts: 0.97 us -> 2.65 us
  transfers between devices with their start and end apart: 2 -> 0, of which waited for: 1 -> 0; matrix products, arithmetic and copies ran while one was open for 5% -> 0% of each run, Pallas kernels for 0% -> 0%
where the time goes in v1:
time: 38.1 us; the launch traced here: 37.7 us
  Pallas kernels  34.5 us (91%)
  local copies, waits for them, and re-layouts  2.65 us (7%)
  between operations  0.64 us (2%)
    pallas_call x1, Pallas kernels, on_device(): pl.pallas_call(kernel, out_shape=(jax.ShapeDtypeStruct((rows, 128), F32),...  34.5 us
    unnamed x2, local copies, waits for them, and re-layouts  2.65 us

profile of v1, /device:TPU:1, one launch (start us, length us, event | category | flops | bytes accessed | tf_op | source)
XLA Modules:
  0.0 37.7 jit_solution(12811888908840271534)
XLA Ops:
  0.6 34.5 %load_transfer.1 = (f32[32,128]{1,0:T(8,128)}, f32[32,128]{1,0:T(8,128)}) custom-call(bf16[8,4,128]{2,1,0:T(4,128)(2,1)} %bitcast.7, bf16[8,8,128,128]{3,2,1,0:T(8,128)(2,1)} %bitcast.4, s32[8,8]{1,0:T(8,128)} %pat_ref.1, s32[1,4]{1,0:T(1,128)} %mask_ref.1, bf16[8,6,128,128]{3,2,1,0:T(8,128)(2,1)} %spline_hbm.1, s32[8,6]{1,0:T(8,128)} %own_ref.1, ...), custom_call_target="tpu_custom_call" | custom-call | tf_op jit(solution)/shard_map/load_transfer/pallas_call | solution.py:277
  35.1 1.3 %copy.12 = f32[1,8,4,128]{3,2,1,0:T(4,128)} copy(f32[1,8,4,128]{3,2,1,0:T(4,128)} %bitcast.6) | data formatting | bytes 32768
  36.4 1.3 %copy.13 = f32[8,4,128]{2,1,0:T(4,128)} copy(f32[8,4,128]{2,1,0:T(4,128)} %bitcast.5) | data formatting | bytes 32768

commit v2 on v1

v2 whole, which is shorter than its diff:
```python
import jax
import jax.numpy as jnp
from jax import lax
from jax.experimental import pallas as pl
from jax.experimental.pallas import tpu as pltpu
from jax.sharding import PartitionSpec as P

MESH = pl.DeviceIdType.MESH
F32 = jnp.float32
BF16 = jnp.bfloat16
MACHS = 8
PANELS = 64
RING = 8
ROWS = 8
NNZ = 8
TARGETS = 6
RHS = 4
CAP = 2
LANES = TARGETS * ROWS * RHS
SERVED = PANELS // 2
SLOTS = SERVED * CAP * RHS


def iota(shape, axis):
    return lax.broadcasted_iota(jnp.int32, shape, axis)


def ones_where(cond):
    return jnp.where(cond, 1.0, 0.0).astype(BF16)


def kernel(
    adj_hbm,
    near_hbm,
    pat_hbm,
    mask_hbm,
    spline_hbm,
    own_hbm,
    loc_hbm,
    inv_hbm,
    loads_ref,
    struct_ref,
    near_ref,
    spline_ref,
    inv_ref,
    own_ref,
    loc_ref,
    pat_ref,
    mask_ref,
    pool,
    mirror,
    relay,
    near_acc,
    mach_buf,
    place,
    pick,
    tab,
    ytab,
    ycomp,
    ztab,
    send_buf,
    recv_buf,
    load_sem,
    halo_send,
    halo_recv,
    relay_send,
    relay_recv,
    pass_send,
    ring_send,
    ring_recv,
    mach_send,
    mach_recv,
    all_send,
    all_recv,
    core_send,
    core_recv,
    next_ready,
    wrap_ready,
    row_near,
    row_far,
    col_ready,
    mach_ready,
    mach_near,
    mach_far,
    row_in,
):
    m = lax.axis_index("mach")
    p = lax.axis_index("panel")
    z = p // RING
    y = p % RING
    core = m % 2
    barrier = pltpu.get_barrier_semaphore()

    def signal(sem, peer):
        pl.semaphore_signal(sem, inc=1, device_id=peer, device_id_type=MESH)

    def row_peer(j):
        return (m, z * RING + (y + j) % RING)

    def column_peer(j):
        return (m, ((z + j) % RING) * RING + y)

    def mach_peer(j):
        return ((m + j) % MACHS, p)

    half = RING // 2
    x = m // 2
    chips = MACHS // 2
    x_up = ((m + 2) % MACHS, p)
    x_down = ((m + MACHS - 2) % MACHS, p)
    other = (m + 1 - 2 * core, p)
    ends_row = (y == RING - 1) & (z < RING - 1)
    opens_row = (y == 0) & (z > 0)
    row_right = (m, z * RING + (y + 1) % RING)
    row_left = (m, z * RING + (y + RING - 1) % RING)

    @pl.when(x < chips - 1)
    def _():
        signal(barrier, x_up)

    @pl.when(x == 0)
    def _():
        signal(barrier, x_down)

    @pl.when(core == 1)
    def _():
        signal(barrier, other)

    @pl.when(y < half)
    def _():
        signal(barrier, row_right)

    @pl.when((y == 0) | (y > half))
    def _():
        signal(barrier, row_left)

    @pl.when(ends_row)
    def _():
        signal(barrier, (m, p + 1))

    def each(low, high, act):
        def step(k, carry):
            act(k)
            return carry

        lax.fori_loop(low, high, step, 0)

    each(z + 1, RING, lambda k: signal(barrier, (m, k * RING + y)))

    pairs = [
        (adj_hbm, pool.at[pl.ds(ROWS, ROWS)]),
        (own_hbm, own_ref),
        (loc_hbm, loc_ref),
        (pat_hbm, pat_ref),
        (mask_hbm, mask_ref),
        (near_hbm, near_ref),
        (spline_hbm, spline_ref),
        (inv_hbm, inv_ref),
    ]
    loads = [
        pltpu.make_async_copy(src, dst, load_sem.at[n]) for n, (src, dst) in enumerate(pairs)
    ]
    adj_load, own_load, loc_load, pat_load, mask_load, near_load, spline_load, inv_load = loads
    for copy in loads:
        copy.start()

    def send(src, dst, send_sem, recv_sem, peer):
        copy = pltpu.make_async_remote_copy(
            src_ref=src,
            dst_ref=dst,
            send_sem=send_sem,
            recv_sem=recv_sem,
            device_id=peer,
            device_id_type=MESH,
        )
        copy.start()
        return copy

    def drain(ref, sem):
        pltpu.make_async_copy(ref, ref, sem).wait()

    row_count = jnp.where(y == 0, opens_row.astype(jnp.int32), jnp.where(y == half, 2, 1))
    mach_count = jnp.where(x == 0, 0, jnp.where(x == chips - 1, 2, 1)) + 1 - core
    count = z + mach_count + row_count

    @pl.when(count > 0)
    def _():
        pl.semaphore_wait(barrier, count)

    adj = pool.at[pl.ds(ROWS, ROWS)]
    after_left = opens_row | ((y > 0) & (y <= half))
    after_right = (y >= half) & (y < RING - 1)
    before_left = y > half
    before_right = (y < half) | ends_row

    @pl.when(z >= RING - 2)
    def _():
        signal(col_ready.at[z], (m, y))

    @pl.when((z == half) | (z == half + 1))
    def _():
        signal(col_ready.at[z], (m, (half - 1) * RING + y))

    @pl.when(after_left)
    def _():
        signal(next_ready.at[1], (m, p - 1))

    @pl.when(after_right)
    def _():
        signal(next_ready.at[0], (m, p + 1))

    @pl.when(z == half - 1)
    def _():
        signal(col_ready.at[z], (m, y))
        signal(col_ready.at[z], (m, RING + y))

    adj_load.wait()

    @pl.when(z >= half)
    def _():
        send(adj, mirror, halo_send.at[0], halo_recv.at[0], (m, p - half * RING))

    def to_left():
        send(adj, pool.at[pl.ds(2 * ROWS, ROWS)], halo_send.at[2], halo_recv.at[2], (m, p - 1))

    def to_right():
        send(adj, pool.at[pl.ds(0, ROWS)], halo_send.at[1], halo_recv.at[1], (m, p + 1))

    pl.when(after_left)(to_left)
    pl.when(after_right)(to_right)

    @pl.when(y == RING - 1)
    def _():
        signal(wrap_ready, row_right)

    @pl.when(core == 0)
    def _():
        signal(mach_ready, other)

    @pl.when(x > 0)
    def _():
        signal(mach_ready, x_down)

    @pl.when(x == chips - 1)
    def _():
        signal(mach_ready, x_up)

    def answer(k):
        told = (
            (z >= RING - 2) & (k == 0)
            | ((z == half) | (z == half + 1)) & (k == half - 1)
            | (z == half - 1) & (k < 2)
        )

        @pl.when(jnp.logical_not(told))
        def _():
            signal(col_ready.at[z], (m, k * RING + y))

    each(0, z, answer)

    @pl.when((z >= 2) & (z < half))
    def _():
        send(adj, relay.at[z - 2], halo_send.at[0], relay_recv.at[z - 2], (m, p - z * RING))

    @pl.when(before_left)
    def _():
        pl.semaphore_wait(next_ready.at[0], 1)
        to_left()

    @pl.when(before_right)
    def _():
        pl.semaphore_wait(next_ready.at[1], 1)
        to_right()

    @pl.when(z < 2)
    def _():
        pl.semaphore_wait(col_ready.at[half - 1], 1)
        send(
            adj, relay.at[z], halo_send.at[0], relay_recv.at[z], (m, p + (half - 1 - z) * RING)
        )

    @pl.when(y == 0)
    def _():
        pl.semaphore_wait(wrap_ready, 1)

    @pl.when(mach_count < 3)
    def _():
        pl.semaphore_wait(mach_ready, 3 - mach_count)

    signal(mach_near, x_up)
    signal(mach_near, x_down)
    signal(mach_near, other)
    signal(row_near, row_right)
    signal(row_near, row_left)

    own_load.wait()
    loc_load.wait()
    own = own_ref[...].astype(F32)
    loc = loc_ref[...].astype(F32)
    lane = iota((ROWS, LANES), 1)
    sub = iota((ROWS, LANES), 0)
    lane_s = lane // (ROWS * RHS)
    lane_i = (lane // RHS) % ROWS
    own_rows = jnp.zeros((ROWS, LANES), F32)
    loc_rows = jnp.zeros((ROWS, LANES), F32)
    for s in range(TARGETS):
        own_rows = jnp.where(lane_s == s, own[:, s : s + 1], own_rows)
        loc_rows = jnp.where(lane_s == s, loc[:, s : s + 1], loc_rows)
    mine = sub == lane_i
    own_lane = jnp.sum(jnp.where(mine, own_rows, 0.0), axis=0, keepdims=True)
    loc_lane = jnp.sum(jnp.where(mine, loc_rows, 0.0), axis=0, keepdims=True)
    same = jnp.zeros((ROWS, LANES), F32)
    for s in range(TARGETS):
        same = same + jnp.where(own[:, s : s + 1] == own_lane, 1.0, 0.0)
    slot = jnp.sum(jnp.where(sub < lane_i, same, 0.0), axis=0, keepdims=True)
    dest = own_lane * CAP + slot
    lane_r = (iota((1, LANES), 1) % RHS).astype(F32)
    chosen = ones_where(iota((PANELS * CAP, LANES), 0).astype(F32) == dest)
    weights = jnp.broadcast_to(
        jnp.where(lane_r == 0.0, loc_lane + 1.0, 0.0), (ROWS, LANES)
    ).astype(BF16)
    tab[...] = lax.dot_general(
        weights, chosen, (((1,), (1,)), ((), ())), preferred_element_type=F32
    )

    owner_row = iota((SLOTS, LANES), 0)
    owner_row = (owner_row // (CAP * RHS)) * (2 * CAP * RHS) + owner_row % (CAP * RHS)
    owner_row = owner_row + core * (CAP * RHS)
    place[...] = ones_where(owner_row.astype(F32) == dest * RHS + lane_r)

    def pass_on(slot, child):
        pltpu.make_async_copy(relay.at[slot], relay.at[slot], relay_recv.at[slot]).wait()
        pl.semaphore_wait(col_ready.at[child], 1)
        send(
            relay.at[slot], mirror, pass_send.at[slot], halo_recv.at[0], (m, child * RING + y)
        )

    @pl.when(z == 3)
    def _():
        pass_on(0, 4)
        pass_on(1, 5)

    @pl.when(z == 0)
    def _():
        pass_on(0, 6)
        pass_on(1, 7)

    pl.semaphore_wait(mach_near, 3)
    signal(mach_far, other)
    pl.semaphore_wait(row_near, 2)
    for j in (1, 2, RING - 2, RING - 1):
        signal(row_far, row_peer(j))

    pat_load.wait()
    near_load.wait()

    @pl.when(p > 0)
    def _():
        drain(mirror, halo_recv.at[1])

    @pl.when(p < PANELS - 1)
    def _():
        drain(mirror, halo_recv.at[2])

    for i in range(ROWS):
        picked = [
            pool[jnp.clip(pat_ref[i, k] - p * ROWS + ROWS, 0, 3 * ROWS - 1)]
            for k in range(2, NNZ)
        ]
        near_acc[RHS * i : RHS * (i + 1), :] = jnp.dot(
            pool[ROWS + i], near_ref[i, 0], preferred_element_type=F32
        ) + jnp.dot(
            jnp.concatenate(picked, axis=1),
            near_ref[i, 2:NNZ].reshape((NNZ - 2) * 128, 128),
            preferred_element_type=F32,
        )

    mask_load.wait()
    row32 = iota((ROWS * RHS, 1), 0)
    gate = jnp.zeros((ROWS * RHS, 1), F32)
    for r in range(RHS):
        gate = jnp.where(row32 % RHS == r, mask_ref[0, r].astype(F32), gate)

    pl.semaphore_wait(row_far, 4)
    for j in range(1, RING):
        send(tab, ytab.at[y], ring_send.at[0], ring_recv.at[0], row_peer(j))
    ytab[y] = tab[...]

    for k in range(1, RING):
        early = (z == 0) & (k in (3, 6, 7)) | (z == 1) & (k == 3) | (z == 3) & (k in (4, 5))

        @pl.when((k > z) & jnp.logical_not(early))
        def _():
            pl.semaphore_wait(col_ready.at[k], 1)

    for j in range(1, RING):
        signal(row_in, column_peer(j))

    pl.semaphore_wait(mach_far, 1)
    drain(mirror, halo_recv.at[0])
    for i in range(ROWS):
        near_acc[RHS * i : RHS * (i + 1), :] += jnp.dot(
            mirror[i], near_ref[i, 1], preferred_element_type=F32
        )
    masked = near_acc[...] * gate
    mach_buf[m] = masked.astype(BF16)
    for j in (4, 3, 5, 2, 6, 1, 7):
        send(mach_buf.at[m], mach_buf.at[m], mach_send, mach_recv, mach_peer(j))
    loads_ref[...] = masked

    spline_load.wait()
    drain(mach_buf.at[pl.ds(0, MACHS - 1)], mach_recv)
    total = mach_buf[0].astype(F32)
    for j in range(1, MACHS):
        total = total + mach_buf[j].astype(F32)
    high = total.astype(BF16).astype(F32)
    both = jnp.concatenate([high, total - high], axis=0)
    row64 = (iota((2 * ROWS * RHS, 128), 0) // RHS) % ROWS
    spread = jnp.concatenate(
        [jnp.where(row64 == i, both, 0.0).astype(BF16) for i in range(ROWS)], axis=1
    )
    contrib = []
    for s in range(TARGETS):
        out = jnp.dot(
            spread,
            spline_ref[:, s].reshape(ROWS * 128, 128),
            preferred_element_type=F32,
        )
        contrib.append((out[: ROWS * RHS] + out[ROWS * RHS :]).astype(BF16))
    packed = jnp.dot(
        place[...], jnp.concatenate(contrib, axis=0), preferred_element_type=F32
    )
    send_buf[...] = packed.astype(BF16).reshape(SERVED, CAP * RHS, 128)

    serves = y % 2 == core
    pl.semaphore_wait(row_in, RING - 1)

    def post(j, carry):
        far = j // (RING // 2)
        side = 1 - 2 * (far % 2)
        to_z = (z + RING // 2 + side * ((far + 1) // 2) + RING) % RING
        to_y = ((y // 2 + 2 + j % (RING // 2)) % (RING // 2)) * 2 + core
        peer = to_z * RING + to_y

        @pl.when(peer != p)
        def _():
            send(send_buf.at[peer // 2], recv_buf.at[p], all_send, all_recv, (m, peer))

        return carry

    lax.fori_loop(0, SERVED, post, 0)

    drain(ytab.at[pl.ds(0, RING - 1)], ring_recv.at[0])
    sub8 = iota((RING, 128), 0)
    comp = jnp.zeros((RING, 128), F32)
    for j in range(RING):
        comp = jnp.where(sub8 == j, ytab[j], comp)
    ycomp[...] = comp
    for j in range(1, RING):
        send(ycomp, ztab.at[z], ring_send.at[1], ring_recv.at[1], column_peer(j))
    ztab[z] = ycomp[...]

    drain(ztab.at[pl.ds(0, RING - 1)], ring_recv.at[1])
    inv_load.wait()

    @pl.when(serves)
    def _():
        recv_buf[p] = send_buf[p // 2]
        lane5 = iota((128, PANELS * CAP * RHS), 1)
        wanted = ones_where(iota((128, PANELS * CAP * RHS), 0) == p * CAP + (lane5 // RHS) % CAP)
        blocks = jnp.dot(
            ztab[...].reshape(PANELS, 128).astype(BF16), wanted, preferred_element_type=F32
        )
        shape = (PANELS, PANELS * CAP * RHS)
        from_panel = iota(shape, 0) == iota(shape, 1) // (CAP * RHS)
        block_lane = jnp.sum(jnp.where(from_panel, blocks, 0.0), axis=0, keepdims=True)
        shape = (ROWS * RHS, PANELS * CAP * RHS)
        row5 = iota(shape, 0)
        col5 = iota(shape, 1)
        pick[...] = ones_where(
            (block_lane == (row5 // RHS + 1).astype(F32)) & (col5 % RHS == row5 % RHS)
        )
        drain(recv_buf.at[pl.ds(0, PANELS - 1)], all_recv)
        found = jnp.dot(
            pick[...],
            recv_buf[...].reshape(PANELS * CAP * RHS, 128),
            preferred_element_type=F32,
        )
        row_block = iota((ROWS * RHS, 128), 0) // RHS
        wide = jnp.concatenate(
            [jnp.where(row_block == t, found, 0.0).astype(BF16) for t in range(ROWS)], axis=1
        )
        struct_ref[...] = jnp.dot(
            wide, inv_ref[...].reshape(ROWS * 128, 128), preferred_element_type=F32
        )
        send(struct_ref, struct_ref, core_send, core_recv, other)
        drain(send_buf.at[pl.ds(0, SERVED - 1)], all_send)
        drain(struct_ref, core_send)

    @pl.when(jnp.logical_not(serves))
    def _():
        drain(send_buf, all_send)
        drain(struct_ref, core_recv)

    drain(mirror, halo_send.at[0])

    @pl.when(p < PANELS - 1)
    def _():
        drain(mirror, halo_send.at[1])

    @pl.when(p > 0)
    def _():
        drain(mirror, halo_send.at[2])

    @pl.when((z == 0) | (z == 3))
    def _():
        drain(mirror, pass_send.at[0])
        drain(mirror, pass_send.at[1])

    for stage, ref in enumerate((ytab, ztab)):
        drain(ref.at[pl.ds(0, RING - 1)], ring_send.at[stage])
    drain(mach_buf.at[pl.ds(0, MACHS - 1)], mach_send)


def hand_on(loads_ref, struct_ref, loads_out, struct_out):
    loads_out[...] = loads_ref[...]
    struct_out[...] = struct_ref[...]


def on_device(adjoint, near, pattern, mask, spline, owner, local, inverse):
    vmem = pl.BlockSpec(memory_space=pltpu.VMEM)
    hbm = pl.BlockSpec(memory_space=pl.ANY)
    rows = ROWS * RHS
    dma = pltpu.SemaphoreType.DMA
    regular = pltpu.SemaphoreType.REGULAR
    loads, struct = pl.pallas_call(
        kernel,
        out_shape=(
            jax.ShapeDtypeStruct((rows, 128), F32),
            jax.ShapeDtypeStruct((rows, 128), F32),
        ),
        in_specs=[hbm] * 8,
        out_specs=(vmem, vmem),
        scratch_shapes=[
            pltpu.VMEM((ROWS, NNZ, 128, 128), BF16),
            pltpu.VMEM((ROWS, TARGETS, 128, 128), BF16),
            pltpu.VMEM((ROWS, 128, 128), BF16),
            pltpu.VMEM((ROWS, TARGETS), jnp.int32),
            pltpu.VMEM((ROWS, TARGETS), jnp.int32),
            pltpu.SMEM((ROWS, NNZ), jnp.int32),
            pltpu.SMEM((1, RHS), jnp.int32),
            pltpu.VMEM((3 * ROWS, RHS, 128), BF16),
            pltpu.VMEM((ROWS, RHS, 128), BF16),
            pltpu.VMEM((2, ROWS, RHS, 128), BF16),
            pltpu.VMEM((rows, 128), F32),
            pltpu.VMEM((MACHS, rows, 128), BF16),
            pltpu.VMEM((SLOTS, LANES), BF16),
            pltpu.VMEM((rows, PANELS * CAP * RHS), BF16),
            pltpu.VMEM((RING, 128), F32),
            pltpu.VMEM((RING, RING, 128), F32),
            pltpu.VMEM((RING, 128), F32),
            pltpu.VMEM((RING, RING, 128), F32),
            pltpu.VMEM((SERVED, CAP * RHS, 128), BF16),
            pltpu.VMEM((PANELS, CAP * RHS, 128), BF16),
            dma((8,)),
            dma((3,)),
            dma((3,)),
            dma((2,)),
            dma((2,)),
            dma((2,)),
            dma((2,)),
            dma((2,)),
            dma,
            dma,
            dma,
            dma,
            dma,
            dma,
            regular((2,)),
            regular,
            regular,
            regular,
            regular((RING,)),
            regular,
            regular,
            regular,
            regular,
        ],
        compiler_params=pltpu.CompilerParams(collective_id=0, has_side_effects=True),
        name="load_transfer",
    )(adjoint[0], near[0], pattern, mask, spline, owner, local, inverse)
    out = jax.ShapeDtypeStruct((rows, 128), F32)
    loads, struct = pl.pallas_call(
        hand_on,
        out_shape=(out, out),
        in_specs=[vmem, vmem],
        out_specs=(vmem, vmem),
        name="hand_on",
    )(loads, struct)
    return loads.reshape(1, ROWS, RHS, 128), struct.reshape(ROWS, RHS, 128)


def solution(mesh):
    in_specs = (
        P("mach", "panel", None, None),
        P("mach", "panel", None, None, None),
        P("panel", None),
        P("mach", None),
        P("panel", None, None, None),
        P("panel", None),
        P("panel", None),
        P("panel", None, None),
    )
    out_specs = (P("mach", "panel", None, None), P("panel", None, None))
    return jax.shard_map(
        on_device, mesh=mesh, in_specs=in_specs, out_specs=out_specs, check_vma=False
    )
```

time: 38.1 us -> 35.5 us (0.932)
  local copies, waits for them, and re-layouts: 2.65 us -> 0 us
    unnamed x2 -> x0, local copies, waits for them, and re-layouts: 2.65 us -> none
    pallas_call x0 -> x1, Pallas kernels: none -> 1.35 us  [on_device(): pl.pallas_call(hand_on, out_shape=(out, out), in_specs=[vmem, vmem], out_...]
    pallas_call x1, Pallas kernels: 34.5 us -> 33.2 us  [on_device(): pl.pallas_call(kernel, out_shape=(jax.ShapeDtypeStruct((rows, 128), F32),...]
where the time goes in v2:
time: 35.5 us; the launch traced here: 35.2 us
  Pallas kernels  34.6 us (97%)
  between operations  0.64 us (2%)
    pallas_call x1, Pallas kernels, on_device(): pl.pallas_call(kernel, out_shape=(jax.ShapeDtypeStruct((rows, 128), F32),...  33.2 us
    pallas_call x1, Pallas kernels, on_device(): pl.pallas_call(hand_on, out_shape=(out, out), in_specs=[vmem, vmem], out_...  1.35 us

profile of v2, /device:TPU:1, one launch (start us, length us, event | category | flops | bytes accessed | tf_op | source)
XLA Modules:
  0.0 35.2 jit_solution(18317667858560512037)
XLA Ops:
  0.6 33.2 %load_transfer.1 = (f32[32,128]{1,0:T(8,128)}, f32[32,128]{1,0:T(8,128)}) custom-call(bf16[8,4,128]{2,1,0:T(4,128)(2,1)} %bitcast.5, bf16[8,8,128,128]{3,2,1,0:T(8,128)(2,1)} %bitcast.4, s32[8,8]{1,0:T(8,128)} %pat_hbm.1, s32[1,4]{1,0:T(1,128)} %mask_hbm.1, bf16[8,6,128,128]{3,2,1,0:T(8,128)(2,1)} %spline_hbm.1, s32[8,6]{1,0:T(8,128)} %own_hbm.1, ...), custom_call_target="tpu_custom_call" | custom-call | tf_op jit(solution)/shard_map/load_transfer/pallas_call | solution.py:536
  33.8 1.3 %hand_on.1 = (f32[32,128]{1,0:T(8,128)}, f32[32,128]{1,0:T(8,128)}) custom-call(f32[32,128]{1,0:T(8,128)} %get-tuple-element.6.loads_ref, f32[32,128]{1,0:T(8,128)} %get-tuple-element.7.struct_ref), custom_call_target="tpu_custom_call" | custom-call | tf_op jit(solution)/shard_map/hand_on/pallas_call | solution.py:593

commit v3 on v2

--- a/solution.py
+++ b/solution.py
@@ -134,7 +134,11 @@
     def _():
         signal(barrier, row_left)
 
-    @pl.when(ends_row)
+    @pl.when(opens_row & (z != half))
+    def _():
+        signal(barrier, (m, p - 1))
+
+    @pl.when(ends_row & (z == half - 1))
     def _():
         signal(barrier, (m, p + 1))
 
@@ -161,8 +165,7 @@
         pltpu.make_async_copy(src, dst, load_sem.at[n]) for n, (src, dst) in enumerate(pairs)
     ]
     adj_load, own_load, loc_load, pat_load, mask_load, near_load, spline_load, inv_load = loads
-    for copy in loads:
-        copy.start()
+    adj_load.start()
 
     def send(src, dst, send_sem, recv_sem, peer):
         copy = pltpu.make_async_remote_copy(
@@ -179,7 +182,9 @@
     def drain(ref, sem):
         pltpu.make_async_copy(ref, ref, sem).wait()
 
-    row_count = jnp.where(y == 0, opens_row.astype(jnp.int32), jnp.where(y == half, 2, 1))
+    row_count = jnp.where(y == 0, 0, jnp.where(y == half, 2, 1))
+    later = (ends_row & (z != half - 1)) | (opens_row & (z == half))
+    row_count = row_count + later.astype(jnp.int32)
     mach_count = jnp.where(x == 0, 0, jnp.where(x == chips - 1, 2, 1)) + 1 - core
     count = z + mach_count + row_count
 
@@ -188,10 +193,10 @@
         pl.semaphore_wait(barrier, count)
 
     adj = pool.at[pl.ds(ROWS, ROWS)]
-    after_left = opens_row | ((y > 0) & (y <= half))
-    after_right = (y >= half) & (y < RING - 1)
-    before_left = y > half
-    before_right = (y < half) | ends_row
+    after_left = ((y > 0) & (y <= half)) | (opens_row & later)
+    after_right = ((y >= half) & (y < RING - 1)) | (ends_row & later)
+    before_left = (y > half) | (opens_row & jnp.logical_not(later))
+    before_right = (y < half) | (ends_row & jnp.logical_not(later))
 
     @pl.when(z >= RING - 2)
     def _():
@@ -228,6 +233,9 @@
 
     pl.when(after_left)(to_left)
     pl.when(after_right)(to_right)
+
+    for copy in loads[1:]:
+        copy.start()
 
     @pl.when(y == RING - 1)
     def _():
@@ -321,7 +329,7 @@
     ).astype(BF16)
     tab[...] = lax.dot_general(
         weights, chosen, (((1,), (1,)), ((), ())), preferred_element_type=F32
-    )
+    )[:1]
 
     owner_row = iota((SLOTS, LANES), 0)
     owner_row = (owner_row // (CAP * RHS)) * (2 * CAP * RHS) + owner_row % (CAP * RHS)
@@ -455,7 +463,7 @@
     comp = jnp.zeros((RING, 128), F32)
     for j in range(RING):
         comp = jnp.where(sub8 == j, ytab[j], comp)
-    ycomp[...] = comp
+    ycomp[...] = comp.astype(BF16)
     for j in range(1, RING):
         send(ycomp, ztab.at[z], ring_send.at[1], ring_recv.at[1], column_peer(j))
     ztab[z] = ycomp[...]
@@ -469,7 +477,7 @@
         lane5 = iota((128, PANELS * CAP * RHS), 1)
         wanted = ones_where(iota((128, PANELS * CAP * RHS), 0) == p * CAP + (lane5 // RHS) % CAP)
         blocks = jnp.dot(
-            ztab[...].reshape(PANELS, 128).astype(BF16), wanted, preferred_element_type=F32
+            ztab[...].astype(F32).reshape(PANELS, 128).astype(BF16), wanted, preferred_element_type=F32
         )
         shape = (PANELS, PANELS * CAP * RHS)
         from_panel = iota(shape, 0) == iota(shape, 1) // (CAP * RHS)
@@ -536,8 +544,8 @@
     loads, struct = pl.pallas_call(
         kernel,
         out_shape=(
-            jax.ShapeDtypeStruct((rows, 128), F32),
-            jax.ShapeDtypeStruct((rows, 128), F32),
+            pltpu.VMEM((rows, 128), F32),
+            pltpu.VMEM((rows, 128), F32),
         ),
         in_specs=[hbm] * 8,
         out_specs=(vmem, vmem),
@@ -556,10 +564,10 @@
             pltpu.VMEM((MACHS, rows, 128), BF16),
             pltpu.VMEM((SLOTS, LANES), BF16),
             pltpu.VMEM((rows, PANELS * CAP * RHS), BF16),
-            pltpu.VMEM((RING, 128), F32),
-            pltpu.VMEM((RING, RING, 128), F32),
-            pltpu.VMEM((RING, 128), F32),
-            pltpu.VMEM((RING, RING, 128), F32),
+            pltpu.VMEM((1, 128), F32),
+            pltpu.VMEM((RING, 1, 128), F32),
+            pltpu.VMEM((RING, 128), BF16),
+            pltpu.VMEM((RING, RING, 128), BF16),
             pltpu.VMEM((SERVED, CAP * RHS, 128), BF16),
             pltpu.VMEM((PANELS, CAP * RHS, 128), BF16),
             dma((8,)),
@@ -596,6 +604,7 @@
         in_specs=[vmem, vmem],
         out_specs=(vmem, vmem),
         name="hand_on",
+        compiler_params=pltpu.CompilerParams(vmem_limit_bytes=1 << 20),
     )(loads, struct)
     return loads.reshape(1, ROWS, RHS, 128), struct.reshape(ROWS, RHS, 128)
 

time: 35.5 us -> 34.1 us (0.961)
  Pallas kernels: 34.6 us -> 33.3 us
    pallas_call x1, Pallas kernels: 1.35 us -> 0.61 us  [on_device(): pl.pallas_call(hand_on, out_shape=(out, out), in_specs=[vmem, vmem], out_...]
    pallas_call x1, Pallas kernels: 33.2 us -> 32.6 us  [on_device(): pl.pallas_call(kernel, out_shape=(pltpu.VMEM((rows, 128), F32), pltpu.VME...]
where the time goes in v3:
time: 34.1 us; the launch traced here: 33.9 us
  Pallas kernels  33.3 us (98%)
  between operations  0.64 us (2%)
    pallas_call x1, Pallas kernels, on_device(): pl.pallas_call(kernel, out_shape=(pltpu.VMEM((rows, 128), F32), pltpu.VME...  32.6 us

profile of v3, /device:TPU:1, one launch (start us, length us, event | category | flops | bytes accessed | tf_op | source)
XLA Modules:
  0.0 33.9 jit_solution(1397281953916528211)
XLA Ops:
  0.6 32.6 %load_transfer.1 = (f32[32,128]{1,0:T(8,128)S(1)}, f32[32,128]{1,0:T(8,128)S(1)}) custom-call(bf16[8,4,128]{2,1,0:T(4,128)(2,1)} %bitcast.5, bf16[8,8,128,128]{3,2,1,0:T(8,128)(2,1)} %bitcast.4, s32[8,8]{1,0:T(8,128)} %pat_hbm.1, s32[1,4]{1,0:T(1,128)} %mask_hbm.1, bf16[8,6,128,128]{3,2,1,0:T(8,128)(2,1)} %spline_hbm.1, s32[8,6]{1,0:T(8,128)} %own_hbm.1, ...), custom_call_target="tpu_custom_call" | custom-call | tf_op jit(solution)/shard_map/load_transfer/pallas_call | solution.py:544
  33.3 0.6 %hand_on.1 = (f32[32,128]{1,0:T(8,128)}, f32[32,128]{1,0:T(8,128)}) custom-call(f32[32,128]{1,0:T(8,128)S(1)} %get-tuple-element.6.loads_ref, f32[32,128]{1,0:T(8,128)S(1)} %get-tuple-element.7.struct_ref), custom_call_target="tpu_custom_call" | custom-call | tf_op jit(solution)/shard_map/hand_on/pallas_call | solution.py:601

commit v4 on v3

--- a/solution.py
+++ b/solution.py
@@ -71,6 +71,7 @@
     mach_send,
     mach_recv,
     all_send,
+    both_send,
     all_recv,
     core_send,
     core_recv,
@@ -89,6 +90,7 @@
     z = p // RING
     y = p % RING
     core = m % 2
+    parity = 1 - core
     barrier = pltpu.get_barrier_semaphore()
 
     def signal(sem, peer):
@@ -333,7 +335,7 @@
 
     owner_row = iota((SLOTS, LANES), 0)
     owner_row = (owner_row // (CAP * RHS)) * (2 * CAP * RHS) + owner_row % (CAP * RHS)
-    owner_row = owner_row + core * (CAP * RHS)
+    owner_row = owner_row + parity * (CAP * RHS)
     place[...] = ones_where(owner_row.astype(F32) == dest * RHS + lane_r)
 
     def pass_on(slot, child):
@@ -440,21 +442,30 @@
     )
     send_buf[...] = packed.astype(BF16).reshape(SERVED, CAP * RHS, 128)
 
-    serves = y % 2 == core
+    serves = y % 2 == parity
+    first = p == 0
     pl.semaphore_wait(row_in, RING - 1)
 
     def post(j, carry):
         far = j // (RING // 2)
         side = 1 - 2 * (far % 2)
         to_z = (z + RING // 2 + side * ((far + 1) // 2) + RING) % RING
-        to_y = ((y // 2 + 2 + j % (RING // 2)) % (RING // 2)) * 2 + core
+        to_y = ((y // 2 + 2 + j % (RING // 2)) % (RING // 2)) * 2 + parity
         peer = to_z * RING + to_y
 
-        @pl.when(peer != p)
+        @pl.when((peer != p) & (peer != 0))
         def _():
             send(send_buf.at[peer // 2], recv_buf.at[p], all_send, all_recv, (m, peer))
 
         return carry
+
+    @pl.when(parity == 0)
+    def _():
+        send(send_buf.at[0], recv_buf.at[p], both_send, all_recv, (m - 1, 0))
+
+        @pl.when(p > 0)
+        def _():
+            send(send_buf.at[0], recv_buf.at[p], all_send, all_recv, (m, 0))
 
     lax.fori_loop(0, SERVED, post, 0)
 
@@ -474,6 +485,9 @@
     @pl.when(serves)
     def _():
         recv_buf[p] = send_buf[p // 2]
+
+    @pl.when(serves | first)
+    def _():
         lane5 = iota((128, PANELS * CAP * RHS), 1)
         wanted = ones_where(iota((128, PANELS * CAP * RHS), 0) == p * CAP + (lane5 // RHS) % CAP)
         blocks = jnp.dot(
@@ -488,7 +502,15 @@
         pick[...] = ones_where(
             (block_lane == (row5 // RHS + 1).astype(F32)) & (col5 % RHS == row5 % RHS)
         )
-        drain(recv_buf.at[pl.ds(0, PANELS - 1)], all_recv)
+
+        @pl.when(serves)
+        def _():
+            drain(recv_buf.at[pl.ds(0, PANELS - 1)], all_recv)
+
+        @pl.when(jnp.logical_not(serves))
+        def _():
+            drain(recv_buf, all_recv)
+
         found = jnp.dot(
             pick[...],
             recv_buf[...].reshape(PANELS * CAP * RHS, 128),
@@ -501,14 +523,29 @@
         struct_ref[...] = jnp.dot(
             wide, inv_ref[...].reshape(ROWS * 128, 128), preferred_element_type=F32
         )
+
+    alone = jnp.logical_not(first)
+
+    @pl.when(serves & alone)
+    def _():
         send(struct_ref, struct_ref, core_send, core_recv, other)
+        drain(struct_ref, core_send)
+
+    @pl.when(jnp.logical_not(serves) & alone)
+    def _():
+        drain(struct_ref, core_recv)
+
+    @pl.when(serves)
+    def _():
         drain(send_buf.at[pl.ds(0, SERVED - 1)], all_send)
-        drain(struct_ref, core_send)
 
     @pl.when(jnp.logical_not(serves))
     def _():
         drain(send_buf, all_send)
-        drain(struct_ref, core_recv)
+
+    @pl.when(parity == 0)
+    def _():
+        drain(send_buf.at[pl.ds(0, 1)], both_send)
 
     drain(mirror, halo_send.at[0])
 
@@ -584,6 +621,7 @@
             dma,
             dma,
             dma,
+            dma,
             regular((2,)),
             regular,
             regular,

time: 34.1 us -> 32.3 us (0.947)
  Pallas kernels: 33.3 us -> 31.3 us
    pallas_call x1, Pallas kernels: 32.6 us -> 30.7 us  [on_device(): pl.pallas_call(kernel, out_shape=(pltpu.VMEM((rows, 128), F32), pltpu.VME...]
where the time goes in v4:
time: 32.3 us; the launch traced here: 32 us
  Pallas kernels  31.3 us (97%)
  between operations  0.64 us (2%)
    pallas_call x1, Pallas kernels, on_device(): pl.pallas_call(kernel, out_shape=(pltpu.VMEM((rows, 128), F32), pltpu.VME...  30.7 us

profile of v4, /device:TPU:1, one launch (start us, length us, event | category | flops | bytes accessed | tf_op | source)
XLA Modules:
  0.0 32.0 jit_solution(5273212368383388855)
XLA Ops:
  0.6 30.7 %load_transfer.1 = (f32[32,128]{1,0:T(8,128)S(1)}, f32[32,128]{1,0:T(8,128)S(1)}) custom-call(bf16[8,4,128]{2,1,0:T(4,128)(2,1)} %bitcast.5, bf16[8,8,128,128]{3,2,1,0:T(8,128)(2,1)} %bitcast.4, s32[8,8]{1,0:T(8,128)} %pat_hbm.1, s32[1,4]{1,0:T(1,128)} %mask_hbm.1, bf16[8,6,128,128]{3,2,1,0:T(8,128)(2,1)} %spline_hbm.1, s32[8,6]{1,0:T(8,128)} %own_hbm.1, ...), custom_call_target="tpu_custom_call" | custom-call | tf_op jit(solution)/shard_map/load_transfer/pallas_call | solution.py:581
  31.4 0.6 %hand_on.1 = (f32[32,128]{1,0:T(8,128)}, f32[32,128]{1,0:T(8,128)}) custom-call(f32[32,128]{1,0:T(8,128)S(1)} %get-tuple-element.6.loads_ref, f32[32,128]{1,0:T(8,128)S(1)} %get-tuple-element.7.struct_ref), custom_call_target="tpu_custom_call" | custom-call | tf_op jit(solution)/shard_map/hand_on/pallas_call | solution.py:639

commit v5 on v4

--- a/solution.py
+++ b/solution.py
@@ -63,7 +63,6 @@
     load_sem,
     halo_send,
     halo_recv,
-    relay_send,
     relay_recv,
     pass_send,
     ring_send,
@@ -204,9 +203,11 @@
     def _():
         signal(col_ready.at[z], (m, y))
 
-    @pl.when((z == half) | (z == half + 1))
-    def _():
-        signal(col_ready.at[z], (m, (half - 1) * RING + y))
+    relayed = (z >= 2) & (z < RING - 2)
+
+    @pl.when(relayed)
+    def _():
+        signal(col_ready.at[z], (m, p - 2 * RING))
 
     @pl.when(after_left)
     def _():
@@ -215,11 +216,6 @@
     @pl.when(after_right)
     def _():
         signal(next_ready.at[0], (m, p + 1))
-
-    @pl.when(z == half - 1)
-    def _():
-        signal(col_ready.at[z], (m, y))
-        signal(col_ready.at[z], (m, RING + y))
 
     adj_load.wait()
 
@@ -256,11 +252,7 @@
         signal(mach_ready, x_up)
 
     def answer(k):
-        told = (
-            (z >= RING - 2) & (k == 0)
-            | ((z == half) | (z == half + 1)) & (k == half - 1)
-            | (z == half - 1) & (k < 2)
-        )
+        told = (z >= RING - 2) & (k == 0) | relayed & (k == z - 2)
 
         @pl.when(jnp.logical_not(told))
         def _():
@@ -284,10 +276,13 @@
 
     @pl.when(z < 2)
     def _():
-        pl.semaphore_wait(col_ready.at[half - 1], 1)
-        send(
-            adj, relay.at[z], halo_send.at[0], relay_recv.at[z], (m, p + (half - 1 - z) * RING)
-        )
+        for k in range(2):
+
+            @pl.when(z == k)
+            def _():
+                pl.semaphore_wait(col_ready.at[k + 2], 1)
+                to = (m, p + 2 * RING)
+                send(adj, relay.at[k], halo_send.at[0], relay_recv.at[k], to)
 
     @pl.when(y == 0)
     def _():
@@ -345,15 +340,18 @@
             relay.at[slot], mirror, pass_send.at[slot], halo_recv.at[0], (m, child * RING + y)
         )
 
+    @pl.when(z == 2)
+    def _():
+        pass_on(0, half)
+
     @pl.when(z == 3)
     def _():
-        pass_on(0, 4)
-        pass_on(1, 5)
+        pass_on(1, half + 1)
 
     @pl.when(z == 0)
     def _():
-        pass_on(0, 6)
-        pass_on(1, 7)
+        pass_on(0, RING - 2)
+        pass_on(1, RING - 1)
 
     pl.semaphore_wait(mach_near, 3)
     signal(mach_far, other)
@@ -397,7 +395,7 @@
     ytab[y] = tab[...]
 
     for k in range(1, RING):
-        early = (z == 0) & (k in (3, 6, 7)) | (z == 1) & (k == 3) | (z == 3) & (k in (4, 5))
+        early = (k == z + 2) & (z < half) | (z == 0) & (k >= RING - 2)
 
         @pl.when((k > z) & jnp.logical_not(early))
         def _():
@@ -443,7 +441,7 @@
     send_buf[...] = packed.astype(BF16).reshape(SERVED, CAP * RHS, 128)
 
     serves = y % 2 == parity
-    first = p == 0
+    first = p < 2
     pl.semaphore_wait(row_in, RING - 1)
 
     def post(j, carry):
@@ -453,22 +451,19 @@
         to_y = ((y // 2 + 2 + j % (RING // 2)) % (RING // 2)) * 2 + parity
         peer = to_z * RING + to_y
 
-        @pl.when((peer != p) & (peer != 0))
+        @pl.when((peer != p) & (peer != parity))
         def _():
             send(send_buf.at[peer // 2], recv_buf.at[p], all_send, all_recv, (m, peer))
 
         return carry
 
-    @pl.when(parity == 0)
-    def _():
-        send(send_buf.at[0], recv_buf.at[p], both_send, all_recv, (m - 1, 0))
-
-        @pl.when(p > 0)
-        def _():
-            send(send_buf.at[0], recv_buf.at[p], all_send, all_recv, (m, 0))
-
-    lax.fori_loop(0, SERVED, post, 0)
-
+    send(send_buf.at[0], recv_buf.at[p], both_send, all_recv, (m + 1 - 2 * core, parity))
+
+    @pl.when(p != parity)
+    def _():
+        send(send_buf.at[0], recv_buf.at[p], all_send, all_recv, (m, parity))
+
+    lax.fori_loop(0, SERVED // 2, post, 0)
     drain(ytab.at[pl.ds(0, RING - 1)], ring_recv.at[0])
     sub8 = iota((RING, 128), 0)
     comp = jnp.zeros((RING, 128), F32)
@@ -478,6 +473,7 @@
     for j in range(1, RING):
         send(ycomp, ztab.at[z], ring_send.at[1], ring_recv.at[1], column_peer(j))
     ztab[z] = ycomp[...]
+    lax.fori_loop(SERVED // 2, SERVED, post, 0)
 
     drain(ztab.at[pl.ds(0, RING - 1)], ring_recv.at[1])
     inv_load.wait()
@@ -543,9 +539,7 @@
     def _():
         drain(send_buf, all_send)
 
-    @pl.when(parity == 0)
-    def _():
-        drain(send_buf.at[pl.ds(0, 1)], both_send)
+    drain(send_buf.at[pl.ds(0, 1)], both_send)
 
     drain(mirror, halo_send.at[0])
 
@@ -557,9 +551,12 @@
     def _():
         drain(mirror, halo_send.at[2])
 
+    @pl.when((z == 0) | (z == 2))
+    def _():
+        drain(mirror, pass_send.at[0])
+
     @pl.when((z == 0) | (z == 3))
     def _():
-        drain(mirror, pass_send.at[0])
         drain(mirror, pass_send.at[1])
 
     for stage, ref in enumerate((ytab, ztab)):
@@ -614,7 +611,6 @@
             dma((2,)),
             dma((2,)),
             dma((2,)),
-            dma((2,)),
             dma,
             dma,
             dma,

time: 32.3 us -> 31.2 us (0.966)
  Pallas kernels: 31.3 us -> 30.4 us
    pallas_call x1, Pallas kernels: 30.7 us -> 29.8 us  [on_device(): pl.pallas_call(kernel, out_shape=(pltpu.VMEM((rows, 128), F32), pltpu.VME...]
where the time goes in v5:
time: 31.2 us; the launch traced here: 31.1 us
  Pallas kernels  30.4 us (97%)
  between operations  0.64 us (2%)
    pallas_call x1, Pallas kernels, on_device(): pl.pallas_call(kernel, out_shape=(pltpu.VMEM((rows, 128), F32), pltpu.VME...  29.8 us

profile of v5, /device:TPU:1, one launch (start us, length us, event | category | flops | bytes accessed | tf_op | source)
XLA Modules:
  0.0 31.1 jit_solution(15688359281202091738)
XLA Ops:
  0.6 29.8 %load_transfer.1 = (f32[32,128]{1,0:T(8,128)S(1)}, f32[32,128]{1,0:T(8,128)S(1)}) custom-call(bf16[8,4,128]{2,1,0:T(4,128)(2,1)} %bitcast.5, bf16[8,8,128,128]{3,2,1,0:T(8,128)(2,1)} %bitcast.4, s32[8,8]{1,0:T(8,128)} %pat_hbm.1, s32[1,4]{1,0:T(1,128)} %mask_hbm.1, bf16[8,6,128,128]{3,2,1,0:T(8,128)(2,1)} %spline_hbm.1, s32[8,6]{1,0:T(8,128)} %own_hbm.1, ...), custom_call_target="tpu_custom_call" | custom-call | tf_op jit(solution)/shard_map/load_transfer/pallas_call | solution.py:578
  30.5 0.6 %hand_on.1 = (f32[32,128]{1,0:T(8,128)}, f32[32,128]{1,0:T(8,128)}) custom-call(f32[32,128]{1,0:T(8,128)S(1)} %get-tuple-element.6.loads_ref, f32[32,128]{1,0:T(8,128)S(1)} %get-tuple-element.7.struct_ref), custom_call_target="tpu_custom_call" | custom-call | tf_op jit(solution)/shard_map/hand_on/pallas_call | solution.py:635

commit v6 on v5

--- a/solution.py
+++ b/solution.py
@@ -70,7 +70,6 @@
     mach_send,
     mach_recv,
     all_send,
-    both_send,
     all_recv,
     core_send,
     core_recv,
@@ -201,13 +200,13 @@
 
     @pl.when(z >= RING - 2)
     def _():
-        signal(col_ready.at[z], (m, y))
+        signal(col_ready.at[z - (RING - 3)], (m, y))
 
     relayed = (z >= 2) & (z < RING - 2)
 
     @pl.when(relayed)
     def _():
-        signal(col_ready.at[z], (m, p - 2 * RING))
+        signal(col_ready.at[0], (m, p - 2 * RING))
 
     @pl.when(after_left)
     def _():
@@ -256,7 +255,7 @@
 
         @pl.when(jnp.logical_not(told))
         def _():
-            signal(col_ready.at[z], (m, k * RING + y))
+            signal(col_ready.at[3], (m, k * RING + y))
 
     each(0, z, answer)
 
@@ -280,7 +279,7 @@
 
             @pl.when(z == k)
             def _():
-                pl.semaphore_wait(col_ready.at[k + 2], 1)
+                pl.semaphore_wait(col_ready.at[0], 1)
                 to = (m, p + 2 * RING)
                 send(adj, relay.at[k], halo_send.at[0], relay_recv.at[k], to)
 
@@ -333,25 +332,25 @@
     owner_row = owner_row + parity * (CAP * RHS)
     place[...] = ones_where(owner_row.astype(F32) == dest * RHS + lane_r)
 
-    def pass_on(slot, child):
+    def pass_on(slot, child, ready):
         pltpu.make_async_copy(relay.at[slot], relay.at[slot], relay_recv.at[slot]).wait()
-        pl.semaphore_wait(col_ready.at[child], 1)
+        pl.semaphore_wait(col_ready.at[ready], 1)
         send(
             relay.at[slot], mirror, pass_send.at[slot], halo_recv.at[0], (m, child * RING + y)
         )
 
     @pl.when(z == 2)
     def _():
-        pass_on(0, half)
+        pass_on(0, half, 0)
 
     @pl.when(z == 3)
     def _():
-        pass_on(1, half + 1)
+        pass_on(1, half + 1, 0)
 
     @pl.when(z == 0)
     def _():
-        pass_on(0, RING - 2)
-        pass_on(1, RING - 1)
+        pass_on(0, RING - 2, 1)
+        pass_on(1, RING - 1, 2)
 
     pl.semaphore_wait(mach_near, 3)
     signal(mach_far, other)
@@ -394,12 +393,11 @@
         send(tab, ytab.at[y], ring_send.at[0], ring_recv.at[0], row_peer(j))
     ytab[y] = tab[...]
 
-    for k in range(1, RING):
-        early = (k == z + 2) & (z < half) | (z == 0) & (k >= RING - 2)
-
-        @pl.when((k > z) & jnp.logical_not(early))
-        def _():
-            pl.semaphore_wait(col_ready.at[k], 1)
+    others = RING - 1 - z - (z < half).astype(jnp.int32) - jnp.where(z == 0, 2, 0)
+
+    @pl.when(others > 0)
+    def _():
+        pl.semaphore_wait(col_ready.at[3], others)
 
     for j in range(1, RING):
         signal(row_in, column_peer(j))
@@ -435,10 +433,14 @@
             preferred_element_type=F32,
         )
         contrib.append((out[: ROWS * RHS] + out[ROWS * RHS :]).astype(BF16))
-    packed = jnp.dot(
-        place[...], jnp.concatenate(contrib, axis=0), preferred_element_type=F32
-    )
-    send_buf[...] = packed.astype(BF16).reshape(SERVED, CAP * RHS, 128)
+    rows = jnp.concatenate(contrib, axis=0)
+
+    def pack(low, high):
+        width = CAP * RHS
+        packed = jnp.dot(place[low * width : high * width], rows, preferred_element_type=F32)
+        send_buf[low:high] = packed.astype(BF16).reshape(high - low, width, 128)
+
+    pack(0, 2)
 
     serves = y % 2 == parity
     first = p < 2
@@ -457,12 +459,13 @@
 
         return carry
 
-    send(send_buf.at[0], recv_buf.at[p], both_send, all_recv, (m + 1 - 2 * core, parity))
+    send(send_buf.at[0], recv_buf.at[p], all_send, all_recv, (m + 1 - 2 * core, parity))
 
     @pl.when(p != parity)
     def _():
         send(send_buf.at[0], recv_buf.at[p], all_send, all_recv, (m, parity))
 
+    pack(2, SERVED)
     lax.fori_loop(0, SERVED // 2, post, 0)
     drain(ytab.at[pl.ds(0, RING - 1)], ring_recv.at[0])
     sub8 = iota((RING, 128), 0)
@@ -533,13 +536,12 @@
 
     @pl.when(serves)
     def _():
-        drain(send_buf.at[pl.ds(0, SERVED - 1)], all_send)
+        drain(send_buf, all_send)
 
     @pl.when(jnp.logical_not(serves))
     def _():
-        drain(send_buf, all_send)
-
-    drain(send_buf.at[pl.ds(0, 1)], both_send)
+        drain(recv_buf.at[pl.ds(0, SERVED + 1)], all_send)
+
 
     drain(mirror, halo_send.at[0])
 
@@ -617,12 +619,11 @@
             dma,
             dma,
             dma,
-            dma,
             regular((2,)),
             regular,
             regular,
             regular,
-            regular((RING,)),
+            regular((4,)),
             regular,
             regular,
             regular,

time: 31.2 us -> 31.1 us (level)
  no operation moved by 1% of the time
where the time goes in v6:
time: 31.1 us; the launch traced here: 31 us
  Pallas kernels  30.3 us (97%)
  between operations  0.64 us (2%)
    pallas_call x1, Pallas kernels, on_device(): pl.pallas_call(kernel, out_shape=(pltpu.VMEM((rows, 128), F32), pltpu.VME...  29.7 us

profile of v6, /device:TPU:1, one launch (start us, length us, event | category | flops | bytes accessed | tf_op | source)
XLA Modules:
  0.0 31.0 jit_solution(11535950966777635740)
XLA Ops:
  0.6 29.7 %load_transfer.1 = (f32[32,128]{1,0:T(8,128)S(1)}, f32[32,128]{1,0:T(8,128)S(1)}) custom-call(bf16[8,4,128]{2,1,0:T(4,128)(2,1)} %bitcast.5, bf16[8,8,128,128]{3,2,1,0:T(8,128)(2,1)} %bitcast.4, s32[8,8]{1,0:T(8,128)} %pat_hbm.1, s32[1,4]{1,0:T(1,128)} %mask_hbm.1, bf16[8,6,128,128]{3,2,1,0:T(8,128)(2,1)} %spline_hbm.1, s32[8,6]{1,0:T(8,128)} %own_hbm.1, ...), custom_call_target="tpu_custom_call" | custom-call | tf_op jit(solution)/shard_map/load_transfer/pallas_call | solution.py:580
  30.4 0.6 %hand_on.1 = (f32[32,128]{1,0:T(8,128)}, f32[32,128]{1,0:T(8,128)}) custom-call(f32[32,128]{1,0:T(8,128)S(1)} %get-tuple-element.6.loads_ref, f32[32,128]{1,0:T(8,128)S(1)} %get-tuple-element.7.struct_ref), custom_call_target="tpu_custom_call" | custom-call | tf_op jit(solution)/shard_map/hand_on/pallas_call | solution.py:636
